TPU v7x, 512 devices: a whole 4x4x16 slice. The times are simulated.
512 devices in a mesh: pix: 64 (over z, y_lo, core), tm: 8 (over y_hi, x).
Axes of the slice: x: 4, y: 4 (y_hi: 2, y_lo: 2; y = y_hi * 2 + y_lo), z: 16, core: 2. Of those that a mesh axis runs over, the one named last changes fastest.
Arguments:
- signal: bfloat16 [16384, 16, 256], P('pix', 'tm'), may hold values from -6 to 6
- lap_tiles: bfloat16 [256, 9, 64, 64], P('pix'), may hold values from -0.25 to 0.25
- neighbours: int32 [256, 9], replicated, may hold values from 0 to 255, as said below
- cheb_weight: bfloat16 [3, 256, 256], replicated, may hold values from -0.21875 to 0.21875
- norm_gain: float32 [256], replicated, may hold values from 0.25 to 1.75
- w_query: bfloat16 [256, 256], replicated, may hold values from -6.5 to 6.5
- w_key: bfloat16 [256, 256], replicated, may hold values from -0.375 to 0.375
- w_value: bfloat16 [256, 256], replicated, may hold values from -0.375 to 0.375
- w_out: bfloat16 [256, 256], replicated, may hold values from -0.375 to 0.375
Outputs:
- result: bfloat16 [16384, 16, 256], P('pix', 'tm')
Inputs may be any that keep to these rules, and one draw needn't show every extreme that they name: `neighbours`: row g lists blocks g - 2, g - 1, g, g + 1, g + 2 in its first five entries (g itself where one of them does not exist); each of the other four entries is one of those five.
All inputs are finite; a program needn't handle non-finite values.
Results may differ from a plain program's by a relative error of at most 0.017.
Values may be sent and summed in bfloat16 or wider, within the bound.
A program may use at most 64 MiB of HBM per device.

v0:
```python
from functools import partial
import math
import jax
import jax.numpy as jnp
from jax import lax
from jax.sharding import PartitionSpec as P

HEADS = 8
reach_blocks = 2


def with_halo(block, sides, width):
    for axis, dim in sides:
        count = lax.axis_size(axis)
        forward = [(i, i + 1) for i in range(count - 1)]
        backward = [(target, source) for source, target in forward]
        low = lax.ppermute(
            lax.slice_in_dim(block, block.shape[dim] - width, None, axis=dim), axis, forward
        )
        high = lax.ppermute(lax.slice_in_dim(block, 0, width, axis=dim), axis, backward)
        block = jnp.concatenate([low, block, high], axis=dim)
    return block


def apply_tiles(tile_blocks, source, sources_at):
    summed = None
    for slot in range(tile_blocks.shape[1]):
        chosen = jnp.take(source, sources_at[:, slot], axis=0, mode="clip")
        product = jnp.einsum(
            "gab,gbf->gaf", tile_blocks[:, slot], chosen, preferred_element_type=jnp.float32
        )
        summed = product if summed is None else summed + product
    return summed


def attend_group(grouped, norm_gain, w_query, w_key, w_value, w_out):
    block = grouped[0]
    count, times, channels = block.shape
    head_dim = channels // HEADS
    flat = block.reshape(count * times, channels).astype(jnp.float32)
    scaling = lax.rsqrt(jnp.mean(flat * flat, axis=1, keepdims=True) + 1e-06)
    normed = (flat * scaling * norm_gain[None, :]).astype(jnp.bfloat16)
    query = jnp.dot(normed, w_query, preferred_element_type=jnp.float32).astype(jnp.bfloat16)
    keys = jnp.dot(normed, w_key, preferred_element_type=jnp.float32).astype(jnp.bfloat16)
    values = jnp.dot(normed, w_value, preferred_element_type=jnp.float32).astype(jnp.bfloat16)
    query = query.reshape(count, times, HEADS, head_dim)
    keys = keys.reshape(count, times, HEADS, head_dim)
    values = values.reshape(count, times, HEADS, head_dim)
    scores = jnp.einsum(
        "pshd,pthd->phst", query, keys, preferred_element_type=jnp.float32
    ) / math.sqrt(head_dim)
    weights = jax.nn.softmax(scores, axis=-1).astype(jnp.bfloat16)
    attended = jnp.einsum(
        "phst,pthd->pshd", weights, values, preferred_element_type=jnp.float32
    ).astype(jnp.bfloat16)
    attended = attended.reshape(count * times, channels)
    output = flat + jnp.dot(attended, w_out, preferred_element_type=jnp.float32)
    return output.astype(jnp.bfloat16).reshape(1, count, times, channels)


def on_device(
    signal, lap_tiles, neighbours, cheb_weight, norm_gain, w_query, w_key, w_value, w_out
):
    pix_count, time_count, channels = signal.shape
    block_count = lap_tiles.shape[0]
    tile_size = lap_tiles.shape[2]
    features = time_count * channels
    blocks = signal.reshape(block_count, tile_size, features)
    first_block = lax.axis_index("pix") * block_count
    own_rows = lax.dynamic_slice_in_dim(neighbours, first_block, block_count, 0)
    sources_at = own_rows - first_block + reach_blocks
    extended = with_halo(blocks, (("pix", 0),), 2)
    first_order = apply_tiles(lap_tiles, extended, sources_at).astype(jnp.bfloat16)
    first_wide = with_halo(first_order, (("pix", 0),), 2)
    second_order = (
        2.0 * apply_tiles(lap_tiles, first_wide, sources_at) - blocks.astype(jnp.float32)
    ).astype(jnp.bfloat16)
    row_count = pix_count * time_count
    plain = signal.reshape(row_count, channels)
    stacked = jnp.concatenate(
        [
            plain,
            first_order.reshape(row_count, channels),
            second_order.reshape(row_count, channels),
        ],
        axis=1,
    )
    mixing = jnp.dot(
        stacked, cheb_weight.reshape(3 * channels, channels), preferred_element_type=jnp.float32
    )
    mixed = (plain.astype(jnp.float32) + jax.nn.silu(mixing)).astype(jnp.bfloat16)
    group_count = lax.axis_size("tm")
    grouped = mixed.reshape(group_count, pix_count // group_count, time_count, channels)
    attend_fn = partial(
        attend_group,
        norm_gain=norm_gain,
        w_query=w_query,
        w_key=w_key,
        w_value=w_value,
        w_out=w_out,
    )
    attended = attend_fn(lax.all_to_all(grouped, "tm", split_axis=0, concat_axis=2, tiled=True))
    returned = lax.all_to_all(attended, "tm", split_axis=2, concat_axis=0, tiled=True)
    return returned.reshape(pix_count, time_count, channels)


def solution(mesh):
    in_specs = (P("pix", "tm", None), P("pix", None, None, None), P(), P(), P(), P(), P(), P(), P())
    out_specs = P("pix", "tm", None)
    return jax.shard_map(
        on_device, mesh=mesh, in_specs=in_specs, out_specs=out_specs, check_vma=False
    )
```

profile of v0, /device:TPU:105, one launch (start us, length us, event | category | flops | bytes accessed | tf_op | source)
XLA Modules:
  0.0 98.8 jit_solution(3153955818766768114)
XLA Ops:
  0.0 1.2 %fusion.106 = (bf16[128,2,256]{2,1,0:T(2,128)(2,1)S(1)}, bf16[128,2,256]{2,1,0:T(2,128)(2,1)S(1)}) fusion(bf16[256,2,256]{2,1,0:T(2,128)(2,1)} %param.9), kind=kLoop, calls=%fused_computation.148 | loop fusion | bytes 524288 | tf_op jit(solution)/shard_map/slice | solution.py:20
  1.3 5.2 %collective-permute-start = (bf16[2,64,512]{2,1,0:T(8,128)(2,1)S(1)}, bf16[2,64,512]{2,1,0:T(8,128)(2,1)S(1)}, u32[]{:S(2)}, u32[]{:S(2)}) collective-permute-start(bf16[2,64,512]{2,1,0:T(8,128)(2,1)S(1)} %slice.91), channel_id=1, source_target_pairs={{0,8},{8,16},{16,24},{24,32},{32,40},{40,48},{48,56},{56,64},{64,7... | collective-permute-start | bytes 393224 | tf_op jit(solution)/shard_map/ppermute | solution.py:17
  6.6 1.9 %collective-permute-start.1 = (bf16[2,64,512]{2,1,0:T(8,128)(2,1)S(1)}, bf16[2,64,512]{2,1,0:T(8,128)(2,1)S(1)}, u32[]{:S(2)}, u32[]{:S(2)}) collective-permute-start(bf16[2,64,512]{2,1,0:T(8,128)(2,1)S(1)} %slice.93), channel_id=1, source_target_pairs={{8,0},{16,8},{24,16},{32,24},{40,32},{48,40},{56,48},{64,56},{72,6... | collective-permute-start | bytes 393224 | tf_op jit(solution)/shard_map/ppermute | solution.py:20
  8.6 0.8 subtract_add_fusion
  9.4 1.1 %reshape.67 = bf16[4,64,512]{2,1,0:T(8,128)(2,1)S(1)} reshape(bf16[256,2,256]{2,1,0:T(2,128)(2,1)} %param.9) | data formatting | bytes 524288 | tf_op jit(solution)/shard_map/reshape | solution.py:68
  10.6 4.4 %collective-permute-done.1 = bf16[2,64,512]{2,1,0:T(8,128)(2,1)S(1)} collective-permute-done((bf16[2,64,512]{2,1,0:T(8,128)(2,1)S(1)}, bf16[2,64,512]{2,1,0:T(8,128)(2,1)S(1)}, u32[]{:S(2)}, u32[]{:S(2)}) %collective-permute-start.1) | collective-permute-done | bytes 131104 | tf_op jit(solution)/shard_map/ppermute | solution.py:20
  15.1 0.6 gather_fusion.7
  15.6 0.6 gather_fusion.6
  16.2 0.2 fusion.43
  16.4 0.2 fusion.47
  16.6 1.3 %gather_fusion.5 = bf16[4,64,512]{2,1,0:T(8,128)(2,1)} fusion(bf16[8,64,512]{2,1,0:T(8,128)(2,1)S(1)} %constant_dynamic-update-slice_fusion, s32[1024]{0:T(1024)S(1)} %get-tuple-element.23), kind=kCustom, calls=%fused_computation.5 | custom fusion | bytes 524304 | tf_op jit(solution)/shard_map/jit(_take)/gather | solution.py:28
  17.9 1.1 %fusion.51 = f32[4,512,64]{1,2,0:T(8,128)S(1)} fusion(bf16[4,64,512]{2,1,0:T(8,128)(2,1)} %gather_fusion.5, bf16[4,9,64,64]{3,2,1,0:T(8,128)(2,1)S(1)} %copy-done.2), kind=kOutput, calls=%fused_computation.82 | convolution fusion | flops 16777216 | bytes 851968 | tf_op jit(solution)/shard_map/gab,gbf->gaf/dot_general | solution.py:29
  19.0 1.3 %gather_fusion.4 = bf16[4,64,512]{2,1,0:T(8,128)(2,1)} fusion(bf16[8,64,512]{2,1,0:T(8,128)(2,1)S(1)} %constant_dynamic-update-slice_fusion, s32[1024]{0:T(1024)S(1)} %get-tuple-element.24), kind=kCustom, calls=%fused_computation.4 | custom fusion | bytes 524304 | tf_op jit(solution)/shard_map/jit(_take)/gather | solution.py:28
  20.3 1.9 %fusion.55 = f32[4,512,64]{1,2,0:T(8,128)} fusion(bf16[4,64,512]{2,1,0:T(8,128)(2,1)} %gather_fusion.4, bf16[4,9,64,64]{3,2,1,0:T(8,128)(2,1)S(1)} %copy-done.2), kind=kOutput, calls=%fused_computation.86 | convolution fusion | flops 16777216 | bytes 851968 | tf_op jit(solution)/shard_map/gab,gbf->gaf/dot_general | solution.py:29
  22.3 1.3 %gather_fusion.3 = bf16[4,64,512]{2,1,0:T(8,128)(2,1)} fusion(bf16[8,64,512]{2,1,0:T(8,128)(2,1)S(1)} %constant_dynamic-update-slice_fusion, s32[1024]{0:T(1024)S(1)} %get-tuple-element.25), kind=kCustom, calls=%fused_computation.3 | custom fusion | bytes 524304 | tf_op jit(solution)/shard_map/jit(_take)/gather | solution.py:28
  23.5 2.0 %fusion.59 = f32[4,512,64]{1,2,0:T(8,128)} fusion(bf16[4,64,512]{2,1,0:T(8,128)(2,1)} %gather_fusion.3, bf16[4,9,64,64]{3,2,1,0:T(8,128)(2,1)S(1)} %copy-done.2), kind=kOutput, calls=%fused_computation.90 | convolution fusion | flops 16777216 | bytes 851968 | tf_op jit(solution)/shard_map/gab,gbf->gaf/dot_general | solution.py:29
  25.5 1.3 %gather_fusion.2 = bf16[4,64,512]{2,1,0:T(8,128)(2,1)} fusion(bf16[8,64,512]{2,1,0:T(8,128)(2,1)S(1)} %constant_dynamic-update-slice_fusion, s32[1024]{0:T(1024)S(1)} %get-tuple-element.26), kind=kCustom, calls=%fused_computation.2 | custom fusion | bytes 524304 | tf_op jit(solution)/shard_map/jit(_take)/gather | solution.py:28
  26.8 2.0 %fusion.63 = f32[4,512,64]{1,2,0:T(8,128)} fusion(bf16[4,64,512]{2,1,0:T(8,128)(2,1)} %gather_fusion.2, bf16[4,9,64,64]{3,2,1,0:T(8,128)(2,1)S(1)} %copy-done.2), kind=kOutput, calls=%fused_computation.94 | convolution fusion | flops 16777216 | bytes 851968 | tf_op jit(solution)/shard_map/gab,gbf->gaf/dot_general | solution.py:29
  28.7 1.3 %gather_fusion.1 = bf16[4,64,512]{2,1,0:T(8,128)(2,1)} fusion(bf16[8,64,512]{2,1,0:T(8,128)(2,1)S(1)} %constant_dynamic-update-slice_fusion, s32[1024]{0:T(1024)S(1)} %get-tuple-element.27), kind=kCustom, calls=%fused_computation.1 | custom fusion | bytes 524304 | tf_op jit(solution)/shard_map/jit(_take)/gather | solution.py:28
  30.0 2.0 %fusion.67 = f32[4,512,64]{1,2,0:T(8,128)} fusion(bf16[4,64,512]{2,1,0:T(8,128)(2,1)} %gather_fusion.1, bf16[4,9,64,64]{3,2,1,0:T(8,128)(2,1)S(1)} %copy-done.2), kind=kOutput, calls=%fused_computation.98 | convolution fusion | flops 16777216 | bytes 851968 | tf_op jit(solution)/shard_map/gab,gbf->gaf/dot_general | solution.py:29
  32.0 1.3 %gather_fusion.8 = bf16[4,64,512]{2,1,0:T(8,128)(2,1)} fusion(bf16[8,64,512]{2,1,0:T(8,128)(2,1)S(1)} %constant_dynamic-update-slice_fusion, s32[1024]{0:T(1024)S(1)} %get-tuple-element.20), kind=kCustom, calls=%fused_computation.8 | custom fusion | bytes 524304 | tf_op jit(solution)/shard_map/jit(_take)/gather | solution.py:28
  33.2 2.0 %fusion.39 = f32[4,512,64]{1,2,0:T(8,128)} fusion(bf16[4,64,512]{2,1,0:T(8,128)(2,1)} %gather_fusion.8, bf16[4,9,64,64]{3,2,1,0:T(8,128)(2,1)S(1)} %copy-done.2), kind=kOutput, calls=%fused_computation.70 | convolution fusion | flops 16777216 | bytes 851968 | tf_op jit(solution)/shard_map/gab,gbf->gaf/dot_general | solution.py:29
  35.2 1.3 %gather_fusion = bf16[4,64,512]{2,1,0:T(8,128)(2,1)} fusion(bf16[8,64,512]{2,1,0:T(8,128)(2,1)S(1)} %constant_dynamic-update-slice_fusion, s32[1024]{0:T(1024)S(1)} %pad_clamp_fusion.8), kind=kCustom, calls=%fused_computation | custom fusion | bytes 524304 | tf_op jit(solution)/shard_map/jit(_take)/gather | solution.py:28
  36.5 2.1 %fusion.23 = bf16[4,64,512]{2,1,0:T(8,128)(2,1)S(1)} fusion(f32[4,512,64]{1,2,0:T(8,128)} %fusion.39, f32[4,512,64]{1,2,0:T(8,128)S(1)} %fusion.43, f32[4,512,64]{1,2,0:T(8,128)S(1)} %fusion.47, f32[4,512,64]{1,2,0:T(8,128)S(1)} %fusion.51, f32[4,512,64]{1,2,0:T(8,128)} %fusion.55, f32[4,512,64]{1,2,0:T(8,128)} %fusion.59, f32[4,512,64]{1,2,0:T(8,128)} %fusion.63, ...), kind=kOutput, calls=%fused_computation.51 | convolution fusion | flops 17956864 | bytes 4784128 | tf_op jit(solution)/shard_map/gab,gbf->gaf/dot_general | solution.py:29
  38.6 1.9 %collective-permute-start.2 = (bf16[2,64,512]{2,1,0:T(8,128)(2,1)S(1)}, bf16[2,64,512]{2,1,0:T(8,128)(2,1)S(1)}, u32[]{:S(2)}, u32[]{:S(2)}) collective-permute-start(bf16[2,64,512]{2,1,0:T(8,128)(2,1)S(1)} %get-tuple-element.5), channel_id=1, source_target_pairs={{0,8},{8,16},{16,24},{24,32},{32,40},{40,48},{48,56},{56,64},{64,7... | collective-permute-start | bytes 393224 | tf_op jit(solution)/shard_map/ppermute | solution.py:17
  40.5 2.4 %collective-permute-start.3 = (bf16[2,64,512]{2,1,0:T(8,128)(2,1)S(1)}, bf16[2,64,512]{2,1,0:T(8,128)(2,1)S(1)}, u32[]{:S(2)}, u32[]{:S(2)}) collective-permute-start(bf16[2,64,512]{2,1,0:T(8,128)(2,1)S(1)} %get-tuple-element.6), channel_id=1, source_target_pairs={{8,0},{16,8},{24,16},{32,24},{40,32},{48,40},{56,48},{64,56},{72,6... | collective-permute-start | bytes 393224 | tf_op jit(solution)/shard_map/ppermute | solution.py:20
  43.0 0.8 reshape.66
  43.8 0.8 reshape.68
  44.5 4.4 %collective-permute-done.3 = bf16[2,64,512]{2,1,0:T(8,128)(2,1)S(1)} collective-permute-done((bf16[2,64,512]{2,1,0:T(8,128)(2,1)S(1)}, bf16[2,64,512]{2,1,0:T(8,128)(2,1)S(1)}, u32[]{:S(2)}, u32[]{:S(2)}) %collective-permute-start.3) | collective-permute-done | bytes 131104 | tf_op jit(solution)/shard_map/ppermute | solution.py:20
  49.0 0.6 gather_fusion.16
  49.6 0.6 gather_fusion.15
  50.1 0.6 gather_fusion.14
  50.7 0.6 gather_fusion.13
  51.3 0.6 gather_fusion.12
  51.9 1.3 %gather_fusion.11 = bf16[4,64,512]{2,1,0:T(8,128)(2,1)} fusion(bf16[8,64,512]{2,1,0:T(8,128)(2,1)S(1)} %pad_maximum_fusion, s32[1024]{0:T(1024)S(1)} %get-tuple-element.26), kind=kCustom, calls=%fused_computation.11 | custom fusion | bytes 524304 | tf_op jit(solution)/shard_map/jit(_take)/gather | solution.py:28
  53.1 1.3 %gather_fusion.10 = bf16[4,64,512]{2,1,0:T(8,128)(2,1)} fusion(bf16[8,64,512]{2,1,0:T(8,128)(2,1)S(1)} %pad_maximum_fusion, s32[1024]{0:T(1024)S(1)} %get-tuple-element.27), kind=kCustom, calls=%fused_computation.10 | custom fusion | bytes 524304 | tf_op jit(solution)/shard_map/jit(_take)/gather | solution.py:28
  54.4 1.3 %gather_fusion.17 = bf16[4,64,512]{2,1,0:T(8,128)(2,1)} fusion(bf16[8,64,512]{2,1,0:T(8,128)(2,1)S(1)} %pad_maximum_fusion, s32[1024]{0:T(1024)S(1)} %get-tuple-element.20), kind=kCustom, calls=%fused_computation.17 | custom fusion | bytes 524304 | tf_op jit(solution)/shard_map/jit(_take)/gather | solution.py:28
  55.7 0.6 gather_fusion.9
  56.2 0.2 fusion.45
  56.4 0.2 fusion.49
  56.7 0.2 fusion.53
  56.9 0.2 fusion.57
  57.1 0.2 fusion.61
  57.3 0.2 fusion.65
  57.9 0.3 fusion.21
  58.4 0.5 copy-done.6
  59.0 0.4 add_convert_fusion
  59.5 13.5 %all_to_all.24 = bf16[8,32,2,256]{3,2,1,0:T(2,128)(2,1)S(1)} all-to-all(bf16[8,32,2,256]{3,2,1,0:T(2,128)(2,1)S(1)} %reshape.71), channel_id=1, replica_groups=mesh['pix'=64,'tm'=8] {'tm'}, dimensions={0} | all-to-all | bytes 524288 | tf_op jit(solution)/shard_map/all_to_all | solution.py:102
  73.2 0.3 copy.68
  73.5 0.4 reshape.78
  73.8 0.3 fusion.36
  74.8 0.2 convolution_convert_fusion.2
  75.0 0.4 reshape.73
  75.5 0.9 convolution_convert_fusion.1
  76.4 1.7 %reshape.74 = bf16[32,16,8,32]{3,2,1,0:T(8,128)(2,1)S(1)} reshape(bf16[512,256]{1,0:T(8,128)(2,1)} %convolution_convert_fusion.1) | data formatting | bytes 524288 | tf_op jit(solution)/shard_map/reshape | solution.py:47
  78.1 0.9 convolution_convert_fusion.3
  79.0 2.4 %reshape.72 = bf16[32,16,8,32]{3,2,1,0:T(8,128)(2,1)} reshape(bf16[512,256]{1,0:T(8,128)(2,1)} %convolution_convert_fusion.3) | data formatting | bytes 524288 | tf_op jit(solution)/shard_map/reshape | solution.py:48
  81.4 2.6 %fusion.107 = (f32[32,8,16]{2,1,0:T(8,128)S(1)}, f32[32,8,16,16]{2,3,1,0:T(8,128)}) fusion(bf16[32,16,8,32]{3,2,1,0:T(8,128)(2,1)S(1)} %reshape.74, bf16[32,16,8,32]{3,2,1,0:T(8,128)(2,1)S(1)} %reshape.73), kind=kOutput, calls=%fused_computation.149 | convolution fusion | flops 4390927 | bytes 802816 | tf_op jit(solution)/shard_map/sub | solution.py:52
  84.0 2.5 %fusion.2 = bf16[32,16,8,32]{3,1,2,0:T(8,128)(2,1)S(1)} fusion(f32[32,8,16,16]{2,3,1,0:T(8,128)} %get-tuple-element.19, bf16[32,16,8,32]{3,2,1,0:T(8,128)(2,1)} %reshape.72, f32[32,8,16]{2,1,0:T(8,128)S(1)} %get-tuple-element.18), kind=kOutput, calls=%fused_computation.24 | convolution fusion | flops 4456448 | bytes 802816 | tf_op jit(solution)/shard_map/phst,pthd->pshd/dot_general | solution.py:53
  86.5 0.3 copy.75
  86.8 0.7 reshape.75
  87.5 0.2 fusion.22
  87.8 10.1 %all_to_all.25 = bf16[1,32,16,256]{3,1,0,2:T(8,128)(2,1)S(1)} all-to-all(bf16[1,32,16,256]{3,1,0,2:T(8,128)(2,1)S(1)} %copy.76), channel_id=1, replica_groups=mesh['pix'=64,'tm'=8] {'tm'}, dimensions={2} | all-to-all | bytes 524288 | tf_op jit(solution)/shard_map/all_to_all | solution.py:103
  97.9 1.0 copy.77
  (51 shorter events, 1.9 us)
Async XLA Ops:
  0.0 58.4 %copy-start = (bf16[3,256,256]{2,1,0:T(8,128)(2,1)S(1)}, bf16[3,256,256]{2,1,0:T(8,128)(2,1)}, u32[]{:S(2)}) copy-start(bf16[3,256,256]{2,1,0:T(8,128)(2,1)} %param.12) | copy-start | bytes 1179652
  0.0 16.2 %copy-start.2 = (bf16[4,9,64,64]{3,2,1,0:T(8,128)(2,1)S(1)}, bf16[4,9,64,64]{3,2,1,0:T(8,128)(2,1)}, u32[]{:S(2)}) copy-start(bf16[4,9,64,64]{3,2,1,0:T(8,128)(2,1)} %param.10) | copy-start | bytes 884740
  1.3 9.2 %collective-permute-start = (bf16[2,64,512]{2,1,0:T(8,128)(2,1)S(1)}, bf16[2,64,512]{2,1,0:T(8,128)(2,1)S(1)}, u32[]{:S(2)}, u32[]{:S(2)}) collective-permute-start(bf16[2,64,512]{2,1,0:T(8,128)(2,1)S(1)} %slice.91), channel_id=1, source_target_pairs={{0,8},{8,16},{16,24},{24,32},{32,40},{40,48},{48,56},{56,64},{64,7... | collective-permute-start | bytes 393224 | tf_op jit(solution)/shard_map/ppermute | solution.py:17
  6.6 8.4 %collective-permute-start.1 = (bf16[2,64,512]{2,1,0:T(8,128)(2,1)S(1)}, bf16[2,64,512]{2,1,0:T(8,128)(2,1)S(1)}, u32[]{:S(2)}, u32[]{:S(2)}) collective-permute-start(bf16[2,64,512]{2,1,0:T(8,128)(2,1)S(1)} %slice.93), channel_id=1, source_target_pairs={{8,0},{16,8},{24,16},{32,24},{40,32},{48,40},{56,48},{64,56},{72,6... | collective-permute-start | bytes 393224 | tf_op jit(solution)/shard_map/ppermute | solution.py:20
  36.5 6.5 %copy-start.1 = (bf16[256,2,256]{2,1,0:T(2,128)(2,1)S(1)}, bf16[256,2,256]{2,1,0:T(2,128)(2,1)}, u32[]{:S(2)}) copy-start(bf16[256,2,256]{2,1,0:T(2,128)(2,1)} %param.9) | copy-start | bytes 786436
  38.6 5.9 %collective-permute-start.2 = (bf16[2,64,512]{2,1,0:T(8,128)(2,1)S(1)}, bf16[2,64,512]{2,1,0:T(8,128)(2,1)S(1)}, u32[]{:S(2)}, u32[]{:S(2)}) collective-permute-start(bf16[2,64,512]{2,1,0:T(8,128)(2,1)S(1)} %get-tuple-element.5), channel_id=1, source_target_pairs={{0,8},{8,16},{16,24},{24,32},{32,40},{40,48},{48,56},{56,64},{64,7... | collective-permute-start | bytes 393224 | tf_op jit(solution)/shard_map/ppermute | solution.py:17
  40.5 8.4 %collective-permute-start.3 = (bf16[2,64,512]{2,1,0:T(8,128)(2,1)S(1)}, bf16[2,64,512]{2,1,0:T(8,128)(2,1)S(1)}, u32[]{:S(2)}, u32[]{:S(2)}) collective-permute-start(bf16[2,64,512]{2,1,0:T(8,128)(2,1)S(1)} %get-tuple-element.6), channel_id=1, source_target_pairs={{8,0},{16,8},{24,16},{32,24},{40,32},{48,40},{56,48},{64,56},{72,6... | collective-permute-start | bytes 393224 | tf_op jit(solution)/shard_map/ppermute | solution.py:20
  56.2 1.1 %copy-start.3 = (bf16[4,64,512]{2,1,0:T(8,128)(2,1)S(1)}, bf16[4,64,512]{2,1,0:T(8,128)(2,1)}, u32[]{:S(2)}) copy-start(bf16[4,64,512]{2,1,0:T(8,128)(2,1)} %gather_fusion.11) | copy-start | bytes 786436
  56.4 1.1 %copy-start.4 = (bf16[4,64,512]{2,1,0:T(8,128)(2,1)S(1)}, bf16[4,64,512]{2,1,0:T(8,128)(2,1)}, u32[]{:S(2)}) copy-start(bf16[4,64,512]{2,1,0:T(8,128)(2,1)} %gather_fusion.10) | copy-start | bytes 786436
  56.7 1.1 %copy-start.5 = (bf16[4,64,512]{2,1,0:T(8,128)(2,1)S(1)}, bf16[4,64,512]{2,1,0:T(8,128)(2,1)}, u32[]{:S(2)}) copy-start(bf16[4,64,512]{2,1,0:T(8,128)(2,1)} %gather_fusion.17) | copy-start | bytes 786436
  57.9 1.0 copy-start.6
  57.9 1.0 %copy-start.7 = (bf16[512,256]{1,0:T(8,128)(2,1)S(1)}, bf16[512,256]{1,0:T(8,128)(2,1)}, u32[]{:S(2)}) copy-start(bf16[512,256]{1,0:T(8,128)(2,1)} %reshape.68) | copy-start | bytes 786436
  59.5 15.1 %copy-start.12 = (f32[256]{0:T(256)S(1)}, f32[256]{0:T(256)}, u32[]{:S(2)}) copy-start(f32[256]{0:T(256)} %param.13) | copy-start | bytes 3076
  73.0 1.8 %copy-start.8 = (bf16[256,256]{1,0:T(8,128)(2,1)S(1)}, bf16[256,256]{1,0:T(8,128)(2,1)}, u32[]{:S(2)}) copy-start(bf16[256,256]{1,0:T(8,128)(2,1)} %param.14) | copy-start | bytes 393220
  73.4 2.0 %copy-start.9 = (bf16[256,256]{1,0:T(8,128)(2,1)S(1)}, bf16[256,256]{1,0:T(8,128)(2,1)}, u32[]{:S(2)}) copy-start(bf16[256,256]{1,0:T(8,128)(2,1)} %param.15) | copy-start | bytes 393220
  74.8 3.3 %copy-start.10 = (bf16[256,256]{1,0:T(8,128)(2,1)S(1)}, bf16[256,256]{1,0:T(8,128)(2,1)}, u32[]{:S(2)}) copy-start(bf16[256,256]{1,0:T(8,128)(2,1)} %param.16) | copy-start | bytes 393220
  86.5 1.0 %copy-start.11 = (bf16[256,256]{1,0:T(8,128)(2,1)S(1)}, bf16[256,256]{1,0:T(8,128)(2,1)}, u32[]{:S(2)}) copy-start(bf16[256,256]{1,0:T(8,128)(2,1)} %param.17) | copy-start | bytes 393220
where the time goes:
time: 99.5 us; the launch traced here: 98.8 us
  local copies, waits for them, and re-layouts  29.7 us (30%)
  blocking collectives  23.5 us (24%)
  matrix products  23.2 us (23%)
  starting transfers between devices  11.5 us (12%)
  waiting for transfers between devices  8.82 us (9%)
  other arithmetic  1.55 us (2%)
    gather x18, local copies, waits for them, and re-layouts, apply_tiles(): chosen = jnp.take(source, sources_at[:, slot], axis=0, mode='clip')  17.2 us
    dot_general x18, matrix products, apply_tiles(): jnp.einsum('gab,gbf->gaf', tile_blocks[:, slot], chosen, preferred_elemen...  15.4 us
    all_to_all x1, blocking collectives, on_device(): lax.all_to_all(grouped, 'tm', split_axis=0, concat_axis=2, tiled=True)  13.5 us
    all_to_all x1, blocking collectives, on_device(): lax.all_to_all(attended, 'tm', split_axis=2, concat_axis=0, tiled=True)  10.1 us
    ppermute x2, waiting for transfers between devices, with_halo(): lax.ppermute(lax.slice_in_dim(block, 0, width, axis=dim), axis, backward)  8.82 us
    ppermute x2, starting transfers between devices, with_halo(): lax.ppermute(lax.slice_in_dim(block, block.shape[dim] - width, None, axis...  7.12 us
    ppermute x2, starting transfers between devices, with_halo(): lax.ppermute(lax.slice_in_dim(block, 0, width, axis=dim), axis, backward)  4.33 us
    sub x1, matrix products, attend_group(): weights = jax.nn.softmax(scores, axis=-1).astype(jnp.bfloat16)  2.57 us
  transfers between devices with their start and end apart: 4, of which 2 were waited for; matrix products, arithmetic and copies ran while one was open for 4% of the time, Pallas kernels for 0%

commit v1 on v0

--- a/solution.py
+++ b/solution.py
@@ -7,6 +7,12 @@
 
 HEADS = 8
 reach_blocks = 2
+
+
+def trade_parts(block, mesh_axis, split, join):
+    pieces = jnp.split(block, lax.axis_size(mesh_axis), axis=split)
+    received = lax.all_to_all(jnp.stack(pieces), mesh_axis, 0, 0)
+    return jnp.concatenate(received, axis=join)
 
 
 def with_halo(block, sides, width):
@@ -100,7 +106,7 @@
         w_out=w_out,
     )
     attended = attend_fn(lax.all_to_all(grouped, "tm", split_axis=0, concat_axis=2, tiled=True))
-    returned = lax.all_to_all(attended, "tm", split_axis=2, concat_axis=0, tiled=True)
+    returned = trade_parts(attended, "tm", 2, 0)
     return returned.reshape(pix_count, time_count, channels)
 
 

time: 99.5 us -> 96.7 us (0.972)
  local copies, waits for them, and re-layouts: 29.7 us -> 27.5 us
    reshape x1, local copies, waits for them, and re-layouts: 1.66 us -> 0.44 us  [attend_group(): keys = keys.reshape(count, times, HEADS, head_dim)]
    reshape x1, local copies, waits for them, and re-layouts: 2.42 us -> 1.41 us  [attend_group(): values = values.reshape(count, times, HEADS, head_dim)]
where the time goes in v1:
time: 96.7 us; the launch traced here: 96.1 us
  local copies, waits for them, and re-layouts  27.5 us (28%)
  blocking collectives  23.5 us (24%)
  matrix products  22.7 us (23%)
  starting transfers between devices  11.5 us (12%)
  waiting for transfers between devices  8.81 us (9%)
  other arithmetic  1.55 us (2%)
    gather x18, local copies, waits for them, and re-layouts, apply_tiles(): chosen = jnp.take(source, sources_at[:, slot], axis=0, mode='clip')  17.2 us
    dot_general x18, matrix products, apply_tiles(): jnp.einsum('gab,gbf->gaf', tile_blocks[:, slot], chosen, preferred_elemen...  15.4 us
    all_to_all x1, blocking collectives, on_device(): lax.all_to_all(grouped, 'tm', split_axis=0, concat_axis=2, tiled=True)  13.5 us
    all_to_all x1, blocking collectives, trade_parts(): received = lax.all_to_all(jnp.stack(pieces), mesh_axis, 0, 0)  10.1 us
    ppermute x2, waiting for transfers between devices, with_halo(): lax.ppermute(lax.slice_in_dim(block, 0, width, axis=dim), axis, backward)  8.8 us
    ppermute x2, starting transfers between devices, with_halo(): lax.ppermute(lax.slice_in_dim(block, block.shape[dim] - width, None, axis...  7.12 us
    ppermute x2, starting transfers between devices, with_halo(): lax.ppermute(lax.slice_in_dim(block, 0, width, axis=dim), axis, backward)  4.33 us
    sub x1, matrix products, attend_group(): weights = jax.nn.softmax(scores, axis=-1).astype(jnp.bfloat16)  2.58 us
  transfers between devices with their start and end apart: 4, of which 2 were waited for; matrix products, arithmetic and copies ran while one was open for 4% of the time, Pallas kernels for 0%

profile of v1, /device:TPU:105, one launch (start us, length us, event | category | flops | bytes accessed | tf_op | source)
XLA Modules:
  0.0 96.1 jit_solution(14192504766297645534)
XLA Ops:
  0.0 1.2 %fusion.114 = (bf16[128,2,256]{2,1,0:T(2,128)(2,1)S(1)}, bf16[128,2,256]{2,1,0:T(2,128)(2,1)S(1)}) fusion(bf16[256,2,256]{2,1,0:T(2,128)(2,1)} %param.9), kind=kLoop, calls=%fused_computation.164 | loop fusion | bytes 524288 | tf_op jit(solution)/shard_map/slice | solution.py:26
  1.3 5.2 %collective-permute-start = (bf16[2,64,512]{2,1,0:T(8,128)(2,1)S(1)}, bf16[2,64,512]{2,1,0:T(8,128)(2,1)S(1)}, u32[]{:S(2)}, u32[]{:S(2)}) collective-permute-start(bf16[2,64,512]{2,1,0:T(8,128)(2,1)S(1)} %slice.91), channel_id=1, source_target_pairs={{0,8},{8,16},{16,24},{24,32},{32,40},{40,48},{48,56},{56,64},{64,7... | collective-permute-start | bytes 393224 | tf_op jit(solution)/shard_map/ppermute | solution.py:23
  6.6 1.9 %collective-permute-start.1 = (bf16[2,64,512]{2,1,0:T(8,128)(2,1)S(1)}, bf16[2,64,512]{2,1,0:T(8,128)(2,1)S(1)}, u32[]{:S(2)}, u32[]{:S(2)}) collective-permute-start(bf16[2,64,512]{2,1,0:T(8,128)(2,1)S(1)} %slice.93), channel_id=1, source_target_pairs={{8,0},{16,8},{24,16},{32,24},{40,32},{48,40},{56,48},{64,56},{72,6... | collective-permute-start | bytes 393224 | tf_op jit(solution)/shard_map/ppermute | solution.py:26
  8.6 0.8 subtract_add_fusion
  9.4 1.1 %reshape.63 = bf16[4,64,512]{2,1,0:T(8,128)(2,1)S(1)} reshape(bf16[256,2,256]{2,1,0:T(2,128)(2,1)} %param.9) | data formatting | bytes 524288 | tf_op jit(solution)/shard_map/reshape | solution.py:74
  10.6 4.4 %collective-permute-done.1 = bf16[2,64,512]{2,1,0:T(8,128)(2,1)S(1)} collective-permute-done((bf16[2,64,512]{2,1,0:T(8,128)(2,1)S(1)}, bf16[2,64,512]{2,1,0:T(8,128)(2,1)S(1)}, u32[]{:S(2)}, u32[]{:S(2)}) %collective-permute-start.1) | collective-permute-done | bytes 131104 | tf_op jit(solution)/shard_map/ppermute | solution.py:26
  15.1 0.6 gather_fusion.7
  15.6 0.6 gather_fusion.6
  16.2 0.2 fusion.43
  16.4 0.2 fusion.47
  16.6 1.3 %gather_fusion.5 = bf16[4,64,512]{2,1,0:T(8,128)(2,1)} fusion(bf16[8,64,512]{2,1,0:T(8,128)(2,1)S(1)} %constant_dynamic-update-slice_fusion, s32[1024]{0:T(1024)S(1)} %get-tuple-element.23), kind=kCustom, calls=%fused_computation.5 | custom fusion | bytes 524304 | tf_op jit(solution)/shard_map/jit(_take)/gather | solution.py:34
  17.9 1.1 %fusion.51 = f32[4,512,64]{1,2,0:T(8,128)S(1)} fusion(bf16[4,64,512]{2,1,0:T(8,128)(2,1)} %gather_fusion.5, bf16[4,9,64,64]{3,2,1,0:T(8,128)(2,1)S(1)} %copy-done.2), kind=kOutput, calls=%fused_computation.82 | convolution fusion | flops 16777216 | bytes 851968 | tf_op jit(solution)/shard_map/gab,gbf->gaf/dot_general | solution.py:35
  19.0 1.3 %gather_fusion.4 = bf16[4,64,512]{2,1,0:T(8,128)(2,1)} fusion(bf16[8,64,512]{2,1,0:T(8,128)(2,1)S(1)} %constant_dynamic-update-slice_fusion, s32[1024]{0:T(1024)S(1)} %get-tuple-element.24), kind=kCustom, calls=%fused_computation.4 | custom fusion | bytes 524304 | tf_op jit(solution)/shard_map/jit(_take)/gather | solution.py:34
  20.3 1.9 %fusion.55 = f32[4,512,64]{1,2,0:T(8,128)} fusion(bf16[4,64,512]{2,1,0:T(8,128)(2,1)} %gather_fusion.4, bf16[4,9,64,64]{3,2,1,0:T(8,128)(2,1)S(1)} %copy-done.2), kind=kOutput, calls=%fused_computation.86 | convolution fusion | flops 16777216 | bytes 851968 | tf_op jit(solution)/shard_map/gab,gbf->gaf/dot_general | solution.py:35
  22.3 1.3 %gather_fusion.3 = bf16[4,64,512]{2,1,0:T(8,128)(2,1)} fusion(bf16[8,64,512]{2,1,0:T(8,128)(2,1)S(1)} %constant_dynamic-update-slice_fusion, s32[1024]{0:T(1024)S(1)} %get-tuple-element.25), kind=kCustom, calls=%fused_computation.3 | custom fusion | bytes 524304 | tf_op jit(solution)/shard_map/jit(_take)/gather | solution.py:34
  23.5 2.0 %fusion.59 = f32[4,512,64]{1,2,0:T(8,128)} fusion(bf16[4,64,512]{2,1,0:T(8,128)(2,1)} %gather_fusion.3, bf16[4,9,64,64]{3,2,1,0:T(8,128)(2,1)S(1)} %copy-done.2), kind=kOutput, calls=%fused_computation.90 | convolution fusion | flops 16777216 | bytes 851968 | tf_op jit(solution)/shard_map/gab,gbf->gaf/dot_general | solution.py:35
  25.5 1.3 %gather_fusion.2 = bf16[4,64,512]{2,1,0:T(8,128)(2,1)} fusion(bf16[8,64,512]{2,1,0:T(8,128)(2,1)S(1)} %constant_dynamic-update-slice_fusion, s32[1024]{0:T(1024)S(1)} %get-tuple-element.26), kind=kCustom, calls=%fused_computation.2 | custom fusion | bytes 524304 | tf_op jit(solution)/shard_map/jit(_take)/gather | solution.py:34
  26.8 2.0 %fusion.63 = f32[4,512,64]{1,2,0:T(8,128)} fusion(bf16[4,64,512]{2,1,0:T(8,128)(2,1)} %gather_fusion.2, bf16[4,9,64,64]{3,2,1,0:T(8,128)(2,1)S(1)} %copy-done.2), kind=kOutput, calls=%fused_computation.94 | convolution fusion | flops 16777216 | bytes 851968 | tf_op jit(solution)/shard_map/gab,gbf->gaf/dot_general | solution.py:35
  28.7 1.3 %gather_fusion.1 = bf16[4,64,512]{2,1,0:T(8,128)(2,1)} fusion(bf16[8,64,512]{2,1,0:T(8,128)(2,1)S(1)} %constant_dynamic-update-slice_fusion, s32[1024]{0:T(1024)S(1)} %get-tuple-element.27), kind=kCustom, calls=%fused_computation.1 | custom fusion | bytes 524304 | tf_op jit(solution)/shard_map/jit(_take)/gather | solution.py:34
  30.0 2.0 %fusion.67 = f32[4,512,64]{1,2,0:T(8,128)} fusion(bf16[4,64,512]{2,1,0:T(8,128)(2,1)} %gather_fusion.1, bf16[4,9,64,64]{3,2,1,0:T(8,128)(2,1)S(1)} %copy-done.2), kind=kOutput, calls=%fused_computation.98 | convolution fusion | flops 16777216 | bytes 851968 | tf_op jit(solution)/shard_map/gab,gbf->gaf/dot_general | solution.py:35
  32.0 1.3 %gather_fusion.8 = bf16[4,64,512]{2,1,0:T(8,128)(2,1)} fusion(bf16[8,64,512]{2,1,0:T(8,128)(2,1)S(1)} %constant_dynamic-update-slice_fusion, s32[1024]{0:T(1024)S(1)} %get-tuple-element.20), kind=kCustom, calls=%fused_computation.8 | custom fusion | bytes 524304 | tf_op jit(solution)/shard_map/jit(_take)/gather | solution.py:34
  33.2 1.9 %fusion.39 = f32[4,512,64]{1,2,0:T(8,128)} fusion(bf16[4,64,512]{2,1,0:T(8,128)(2,1)} %gather_fusion.8, bf16[4,9,64,64]{3,2,1,0:T(8,128)(2,1)S(1)} %copy-done.2), kind=kOutput, calls=%fused_computation.70 | convolution fusion | flops 16777216 | bytes 851968 | tf_op jit(solution)/shard_map/gab,gbf->gaf/dot_general | solution.py:35
  35.2 1.3 %gather_fusion = bf16[4,64,512]{2,1,0:T(8,128)(2,1)} fusion(bf16[8,64,512]{2,1,0:T(8,128)(2,1)S(1)} %constant_dynamic-update-slice_fusion, s32[1024]{0:T(1024)S(1)} %pad_clamp_fusion.8), kind=kCustom, calls=%fused_computation | custom fusion | bytes 524304 | tf_op jit(solution)/shard_map/jit(_take)/gather | solution.py:34
  36.4 2.1 %fusion.23 = bf16[4,64,512]{2,1,0:T(8,128)(2,1)S(1)} fusion(f32[4,512,64]{1,2,0:T(8,128)} %fusion.39, f32[4,512,64]{1,2,0:T(8,128)S(1)} %fusion.43, f32[4,512,64]{1,2,0:T(8,128)S(1)} %fusion.47, f32[4,512,64]{1,2,0:T(8,128)S(1)} %fusion.51, f32[4,512,64]{1,2,0:T(8,128)} %fusion.55, f32[4,512,64]{1,2,0:T(8,128)} %fusion.59, f32[4,512,64]{1,2,0:T(8,128)} %fusion.63, ...), kind=kOutput, calls=%fused_computation.51 | convolution fusion | flops 17956864 | bytes 4784128 | tf_op jit(solution)/shard_map/gab,gbf->gaf/dot_general | solution.py:35
  38.6 1.9 %collective-permute-start.2 = (bf16[2,64,512]{2,1,0:T(8,128)(2,1)S(1)}, bf16[2,64,512]{2,1,0:T(8,128)(2,1)S(1)}, u32[]{:S(2)}, u32[]{:S(2)}) collective-permute-start(bf16[2,64,512]{2,1,0:T(8,128)(2,1)S(1)} %get-tuple-element.5), channel_id=1, source_target_pairs={{0,8},{8,16},{16,24},{24,32},{32,40},{40,48},{48,56},{56,64},{64,7... | collective-permute-start | bytes 393224 | tf_op jit(solution)/shard_map/ppermute | solution.py:23
  40.5 2.4 %collective-permute-start.3 = (bf16[2,64,512]{2,1,0:T(8,128)(2,1)S(1)}, bf16[2,64,512]{2,1,0:T(8,128)(2,1)S(1)}, u32[]{:S(2)}, u32[]{:S(2)}) collective-permute-start(bf16[2,64,512]{2,1,0:T(8,128)(2,1)S(1)} %get-tuple-element.6), channel_id=1, source_target_pairs={{8,0},{16,8},{24,16},{32,24},{40,32},{48,40},{56,48},{64,56},{72,6... | collective-permute-start | bytes 393224 | tf_op jit(solution)/shard_map/ppermute | solution.py:26
  42.9 0.8 reshape.62
  43.7 0.8 reshape.64
  44.5 4.4 %collective-permute-done.3 = bf16[2,64,512]{2,1,0:T(8,128)(2,1)S(1)} collective-permute-done((bf16[2,64,512]{2,1,0:T(8,128)(2,1)S(1)}, bf16[2,64,512]{2,1,0:T(8,128)(2,1)S(1)}, u32[]{:S(2)}, u32[]{:S(2)}) %collective-permute-start.3) | collective-permute-done | bytes 131104 | tf_op jit(solution)/shard_map/ppermute | solution.py:26
  49.0 0.6 gather_fusion.16
  49.6 0.6 gather_fusion.15
  50.1 0.6 gather_fusion.14
  50.7 0.6 gather_fusion.13
  51.3 0.6 gather_fusion.12
  51.8 1.3 %gather_fusion.11 = bf16[4,64,512]{2,1,0:T(8,128)(2,1)} fusion(bf16[8,64,512]{2,1,0:T(8,128)(2,1)S(1)} %pad_maximum_fusion, s32[1024]{0:T(1024)S(1)} %get-tuple-element.26), kind=kCustom, calls=%fused_computation.11 | custom fusion | bytes 524304 | tf_op jit(solution)/shard_map/jit(_take)/gather | solution.py:34
  53.1 1.3 %gather_fusion.10 = bf16[4,64,512]{2,1,0:T(8,128)(2,1)} fusion(bf16[8,64,512]{2,1,0:T(8,128)(2,1)S(1)} %pad_maximum_fusion, s32[1024]{0:T(1024)S(1)} %get-tuple-element.27), kind=kCustom, calls=%fused_computation.10 | custom fusion | bytes 524304 | tf_op jit(solution)/shard_map/jit(_take)/gather | solution.py:34
  54.4 1.3 %gather_fusion.17 = bf16[4,64,512]{2,1,0:T(8,128)(2,1)} fusion(bf16[8,64,512]{2,1,0:T(8,128)(2,1)S(1)} %pad_maximum_fusion, s32[1024]{0:T(1024)S(1)} %get-tuple-element.20), kind=kCustom, calls=%fused_computation.17 | custom fusion | bytes 524304 | tf_op jit(solution)/shard_map/jit(_take)/gather | solution.py:34
  55.7 0.6 gather_fusion.9
  56.2 0.2 fusion.45
  56.5 0.2 fusion.49
  56.9 0.2 fusion.57
  57.1 0.2 fusion.61
  57.3 0.2 fusion.65
  57.5 0.2 fusion.69
  57.9 0.3 fusion.21
  58.4 0.5 copy-done.6
  59.0 0.4 add_convert_fusion
  59.5 13.5 %all_to_all.14 = bf16[8,32,2,256]{3,2,1,0:T(2,128)(2,1)S(1)} all-to-all(bf16[8,32,2,256]{3,2,1,0:T(2,128)(2,1)S(1)} %reshape.67), channel_id=1, replica_groups=mesh['pix'=64,'tm'=8] {'tm'}, dimensions={0} | all-to-all | bytes 524288 | tf_op jit(solution)/shard_map/all_to_all | solution.py:108
  73.1 0.3 copy.64
  73.4 0.4 reshape.73
  73.8 0.3 fusion.36
  74.8 0.2 convolution_convert_fusion.2
  75.0 0.4 reshape.69
  75.4 0.2 convolution_convert_fusion.1
  75.7 0.4 reshape.70
  76.1 1.1 %convolution_convert_fusion.3 = bf16[512,256]{1,0:T(8,128)(2,1)S(1)} fusion(bf16[512,256]{1,0:T(8,128)(2,1)S(1)} %multiply_convert_fusion, bf16[256,256]{1,0:T(8,128)(2,1)} %param.16), kind=kOutput, calls=%fused_computation.49 | convolution fusion | flops 67239936 | bytes 655360 | tf_op jit(solution)/shard_map/dot_general | solution.py:51
  77.3 1.4 %reshape.68 = bf16[32,16,8,32]{3,2,1,0:T(8,128)(2,1)} reshape(bf16[512,256]{1,0:T(8,128)(2,1)S(1)} %convolution_convert_fusion.3) | data formatting | bytes 524288 | tf_op jit(solution)/shard_map/reshape | solution.py:54
  78.7 2.6 %fusion.115 = (f32[32,8,16]{2,1,0:T(8,128)S(1)}, f32[32,8,16,16]{2,3,1,0:T(8,128)}) fusion(bf16[32,16,8,32]{3,2,1,0:T(8,128)(2,1)S(1)} %reshape.70, bf16[32,16,8,32]{3,2,1,0:T(8,128)(2,1)S(1)} %reshape.69), kind=kOutput, calls=%fused_computation.165 | convolution fusion | flops 4390927 | bytes 802816 | tf_op jit(solution)/shard_map/sub | solution.py:58
  81.2 2.5 %fusion.2 = bf16[32,16,8,32]{3,1,2,0:T(8,128)(2,1)S(1)} fusion(f32[32,8,16,16]{2,3,1,0:T(8,128)} %get-tuple-element.19, bf16[32,16,8,32]{3,2,1,0:T(8,128)(2,1)} %reshape.68, f32[32,8,16]{2,1,0:T(8,128)S(1)} %get-tuple-element.18), kind=kOutput, calls=%fused_computation.24 | convolution fusion | flops 4456448 | bytes 802816 | tf_op jit(solution)/shard_map/phst,pthd->pshd/dot_general | solution.py:59
  83.7 0.3 copy.71
  84.0 0.7 reshape.71
  84.7 0.2 fusion.22
  85.3 10.1 %all_to_all.15 = bf16[8,1,32,2,256]{4,3,2,1,0:T(2,128)(2,1)S(1)} all-to-all(bf16[8,1,32,2,256]{4,3,2,1,0:T(2,128)(2,1)S(1)} %fusion.91), channel_id=1, replica_groups=mesh['pix'=64,'tm'=8] {'tm'}, dimensions={0} | all-to-all | bytes 524288 | tf_op jit(solution)/shard_map/all_to_all | solution.py:14
  95.4 0.7 copy.114
  (56 shorter events, 2.1 us)
Async XLA Ops:
  0.0 58.4 %copy-start = (bf16[3,256,256]{2,1,0:T(8,128)(2,1)S(1)}, bf16[3,256,256]{2,1,0:T(8,128)(2,1)}, u32[]{:S(2)}) copy-start(bf16[3,256,256]{2,1,0:T(8,128)(2,1)} %param.12) | copy-start | bytes 1179652
  0.0 16.2 %copy-start.2 = (bf16[4,9,64,64]{3,2,1,0:T(8,128)(2,1)S(1)}, bf16[4,9,64,64]{3,2,1,0:T(8,128)(2,1)}, u32[]{:S(2)}) copy-start(bf16[4,9,64,64]{3,2,1,0:T(8,128)(2,1)} %param.10) | copy-start | bytes 884740
  1.3 9.2 %collective-permute-start = (bf16[2,64,512]{2,1,0:T(8,128)(2,1)S(1)}, bf16[2,64,512]{2,1,0:T(8,128)(2,1)S(1)}, u32[]{:S(2)}, u32[]{:S(2)}) collective-permute-start(bf16[2,64,512]{2,1,0:T(8,128)(2,1)S(1)} %slice.91), channel_id=1, source_target_pairs={{0,8},{8,16},{16,24},{24,32},{32,40},{40,48},{48,56},{56,64},{64,7... | collective-permute-start | bytes 393224 | tf_op jit(solution)/shard_map/ppermute | solution.py:23
  6.6 8.4 %collective-permute-start.1 = (bf16[2,64,512]{2,1,0:T(8,128)(2,1)S(1)}, bf16[2,64,512]{2,1,0:T(8,128)(2,1)S(1)}, u32[]{:S(2)}, u32[]{:S(2)}) collective-permute-start(bf16[2,64,512]{2,1,0:T(8,128)(2,1)S(1)} %slice.93), channel_id=1, source_target_pairs={{8,0},{16,8},{24,16},{32,24},{40,32},{48,40},{56,48},{64,56},{72,6... | collective-permute-start | bytes 393224 | tf_op jit(solution)/shard_map/ppermute | solution.py:26
  36.4 6.5 %copy-start.1 = (bf16[256,2,256]{2,1,0:T(2,128)(2,1)S(1)}, bf16[256,2,256]{2,1,0:T(2,128)(2,1)}, u32[]{:S(2)}) copy-start(bf16[256,2,256]{2,1,0:T(2,128)(2,1)} %param.9) | copy-start | bytes 786436
  38.6 5.9 %collective-permute-start.2 = (bf16[2,64,512]{2,1,0:T(8,128)(2,1)S(1)}, bf16[2,64,512]{2,1,0:T(8,128)(2,1)S(1)}, u32[]{:S(2)}, u32[]{:S(2)}) collective-permute-start(bf16[2,64,512]{2,1,0:T(8,128)(2,1)S(1)} %get-tuple-element.5), channel_id=1, source_target_pairs={{0,8},{8,16},{16,24},{24,32},{32,40},{40,48},{48,56},{56,64},{64,7... | collective-permute-start | bytes 393224 | tf_op jit(solution)/shard_map/ppermute | solution.py:23
  40.5 8.4 %collective-permute-start.3 = (bf16[2,64,512]{2,1,0:T(8,128)(2,1)S(1)}, bf16[2,64,512]{2,1,0:T(8,128)(2,1)S(1)}, u32[]{:S(2)}, u32[]{:S(2)}) collective-permute-start(bf16[2,64,512]{2,1,0:T(8,128)(2,1)S(1)} %get-tuple-element.6), channel_id=1, source_target_pairs={{8,0},{16,8},{24,16},{32,24},{40,32},{48,40},{56,48},{64,56},{72,6... | collective-permute-start | bytes 393224 | tf_op jit(solution)/shard_map/ppermute | solution.py:26
  56.2 1.1 %copy-start.3 = (bf16[4,64,512]{2,1,0:T(8,128)(2,1)S(1)}, bf16[4,64,512]{2,1,0:T(8,128)(2,1)}, u32[]{:S(2)}) copy-start(bf16[4,64,512]{2,1,0:T(8,128)(2,1)} %gather_fusion.11) | copy-start | bytes 786436
  56.4 1.1 %copy-start.4 = (bf16[4,64,512]{2,1,0:T(8,128)(2,1)S(1)}, bf16[4,64,512]{2,1,0:T(8,128)(2,1)}, u32[]{:S(2)}) copy-start(bf16[4,64,512]{2,1,0:T(8,128)(2,1)} %gather_fusion.10) | copy-start | bytes 786436
  56.7 1.1 %copy-start.5 = (bf16[4,64,512]{2,1,0:T(8,128)(2,1)S(1)}, bf16[4,64,512]{2,1,0:T(8,128)(2,1)}, u32[]{:S(2)}) copy-start(bf16[4,64,512]{2,1,0:T(8,128)(2,1)} %gather_fusion.17) | copy-start | bytes 786436
  57.9 1.0 copy-start.6
  57.9 1.0 %copy-start.7 = (bf16[512,256]{1,0:T(8,128)(2,1)S(1)}, bf16[512,256]{1,0:T(8,128)(2,1)}, u32[]{:S(2)}) copy-start(bf16[512,256]{1,0:T(8,128)(2,1)} %reshape.64) | copy-start | bytes 786436
  59.5 15.1 %copy-start.11 = (f32[256]{0:T(256)S(1)}, f32[256]{0:T(256)}, u32[]{:S(2)}) copy-start(f32[256]{0:T(256)} %param.13) | copy-start | bytes 3076
  73.0 1.8 %copy-start.8 = (bf16[256,256]{1,0:T(8,128)(2,1)S(1)}, bf16[256,256]{1,0:T(8,128)(2,1)}, u32[]{:S(2)}) copy-start(bf16[256,256]{1,0:T(8,128)(2,1)} %param.14) | copy-start | bytes 393220
  73.4 2.0 %copy-start.9 = (bf16[256,256]{1,0:T(8,128)(2,1)S(1)}, bf16[256,256]{1,0:T(8,128)(2,1)}, u32[]{:S(2)}) copy-start(bf16[256,256]{1,0:T(8,128)(2,1)} %param.15) | copy-start | bytes 393220
  83.7 1.0 %copy-start.10 = (bf16[256,256]{1,0:T(8,128)(2,1)S(1)}, bf16[256,256]{1,0:T(8,128)(2,1)}, u32[]{:S(2)}) copy-start(bf16[256,256]{1,0:T(8,128)(2,1)} %param.17) | copy-start | bytes 393220
